TPU v7x, 32 devices: a whole 2x2x4 slice. The times are simulated.
32 devices in a mesh: obs: 4 (over y, x), par: 8 (over z, core).
Axes of the slice: x: 2, y: 2, z: 4, core: 2. Of those that a mesh axis runs over, the one named last changes fastest.
Arguments:
- jacobian: bfloat16 [2048, 32768], P('obs', 'par'), may hold values from -0.03125 to 0.03125
- probes: bfloat16 [32768, 256], P('par'), may hold values from -6 to 6
- coeffs: bfloat16 [256, 3, 128, 128], P('par'), may hold values from -0.3125 to 0.3125
- offsets: int32 [256, 2], P('par'), may hold values from -4 to 4
Outputs:
- ritz_basis: bfloat16 [32768, 256], P('par')
- basis_image: bfloat16 [32768, 256], P('par')
- ritz_matrix: float32 [256, 256], replicated
All inputs are finite; a program needn't handle non-finite values.
Results may differ from a plain program's by a relative error of at most 0.015.
Values may be sent and summed in bfloat16 or wider, within the bound.
A program may use at most 128 MiB of HBM per device.

v0:
```python
import jax
import jax.numpy as jnp
from jax import lax
from jax.sharding import PartitionSpec as P

BLK = 128
REACH = 4


def shifted(value, axis, by):
    count = lax.axis_size(axis)
    pairs = [(i, i + by) for i in range(count) if 0 <= i + by < count]
    return lax.ppermute(value, axis, pairs)


def extended_2(cells, sides, width):
    for axis, dim in sides:
        count = lax.axis_size(axis)
        ends = count - 1
        head = lax.slice_in_dim(cells, 0, width, axis=dim)
        tail = lax.slice_in_dim(cells, cells.shape[dim] - width, cells.shape[dim], axis=dim)
        cells = jnp.concatenate(
            [
                lax.ppermute(tail, axis, [(i, (i + 1) % count) for i in range(ends)]),
                cells,
                lax.ppermute(head, axis, [((i + 1) % count, i) for i in range(ends)]),
            ],
            axis=dim,
        )
    return cells


def block_index(offsets):
    count = offsets.shape[0]
    full_offsets = jnp.concatenate([jnp.zeros((count, 1), jnp.int32), offsets], axis=1)
    return jnp.arange(count, dtype=jnp.int32)[:, None] + REACH + full_offsets


def prior_forward(extended, coeffs, offsets):
    width = extended.shape[1]
    positions = block_index(offsets)
    padded = extended.reshape(-1, BLK, width)
    picked = padded[positions]
    result = jnp.einsum("bjrc,bjcn->brn", coeffs, picked, preferred_element_type=jnp.float32)
    return result.reshape(-1, width).astype(jnp.bfloat16)


def prior_adjoint(values, coeffs, offsets):
    width = values.shape[1]
    count = offsets.shape[0]
    positions = block_index(offsets)
    blocks = values.reshape(count, BLK, width)
    contrib = jnp.einsum("bjcr,bcn->bjrn", coeffs, blocks, preferred_element_type=jnp.float32)
    accumulated = jnp.zeros((count + 2 * REACH, BLK, width), jnp.float32).at[positions].add(contrib)
    inner = accumulated[REACH : REACH + count]
    from_upper = shifted(accumulated[:REACH].astype(jnp.bfloat16), "par", -1).astype(jnp.float32)
    from_lower = shifted(accumulated[REACH + count :].astype(jnp.bfloat16), "par", 1).astype(
        jnp.float32
    )
    inner = inner.at[count - REACH :].add(from_upper)
    inner = inner.at[:REACH].add(from_lower)
    return inner.reshape(-1, width)


def body(jacobian, probes, coeffs, offsets):
    total_par = jacobian.shape[1] * lax.axis_size("par")
    total_obs = jacobian.shape[0] * lax.axis_size("obs")
    probe_halo = extended_2(probes, (("par", 0),), REACH * BLK)
    sampled = prior_forward(probe_halo, coeffs, offsets)
    forward_part = jnp.dot(jacobian, sampled, preferred_element_type=jnp.float32)
    forward = lax.psum(forward_part, "par").astype(jnp.bfloat16)
    adjoint_part = lax.dot_general(
        jacobian, forward, (((0,), (0,)), ((), ())), preferred_element_type=jnp.float32
    )
    adjoint_cols = lax.psum_scatter(
        adjoint_part.astype(jnp.bfloat16), "obs", scatter_dimension=1, tiled=True
    )
    sample_cols = prior_adjoint(adjoint_cols, coeffs, offsets)
    range_sample = lax.all_gather(
        sample_cols.astype(jnp.bfloat16), "obs", axis=1, tiled=True
    ).astype(sample_cols.dtype)
    gram_part = jnp.dot(range_sample.T, range_sample, precision=lax.Precision.HIGHEST)
    gram_matrix = lax.psum(gram_part, "par") / total_par
    lower_factor = jnp.linalg.cholesky(gram_matrix)
    solved = lax.linalg.triangular_solve(
        lower_factor, range_sample, left_side=False, lower=True, transpose_a=True
    )
    ritz_basis = solved.astype(jnp.bfloat16)
    basis_halo = extended_2(ritz_basis, (("par", 0),), REACH * BLK)
    basis_image = prior_forward(basis_halo, coeffs, offsets)
    projected_part = jnp.dot(jacobian, basis_image, preferred_element_type=jnp.float32)
    projected = lax.psum(projected_part, "par")
    ritz_part = jnp.dot(projected.T, projected, precision=lax.Precision.HIGHEST)
    ritz_matrix = lax.psum(ritz_part.astype(jnp.bfloat16), "obs").astype(jnp.float32) / total_obs
    return (ritz_basis, basis_image, ritz_matrix)


def solution(mesh):
    return jax.shard_map(
        body,
        mesh=mesh,
        in_specs=(P("obs", "par"), P("par", None), P("par", None, None, None), P("par", None)),
        out_specs=(P("par", None), P("par", None), P()),
        check_vma=False,
    )
```

profile of v0, /device:TPU:0, one launch (start us, length us, event | category | flops | bytes accessed | tf_op | source)
XLA Modules:
  0.0 453.3 jit_solution(15713091920157657930)
XLA Ops:
  7.2 2.0 fusion.16
  9.2 3.1 collective-permute-start
  12.3 1.3 collective-permute-start.1
  14.5 3.0 collective-permute-done.1
  17.6 3.4 pad_maximum_fusion.1
  21.0 7.8 %gather_fusion = bf16[96,128,256]{2,1,0:T(8,128)(2,1)} fusion(bf16[40,128,256]{2,1,0:T(8,128)(2,1)} %bitcast.86, s32[1024]{0:T(1024)S(1)} %pad_clamp_fusion), kind=kCustom, calls=%fused_computation | custom fusion | bytes 12583296 | tf_op jit(solution)/shard_map/gather | solution.py:43
  28.8 4.2 bitcast_convert_fusion.1
  33.0 2.1 convolution_bitcast_fusion.1
  35.1 37.8 %all-reduce.12 = bf16[512,256]{0,1:T(8,128)(2,1)} all-reduce(f32[512,256]{0,1:T(8,128)} %convolution_bitcast_fusion.1), channel_id=1, replica_groups=mesh['obs'=4,'par'=8] {'par'}, use_global_device_ids=true, to_apply=%region_0.0 | all-reduce | flops 131072 | bytes 786432 | tf_op jit(solution)/shard_map/psum | solution.py:71
  72.9 4.9 %fusion = bf16[4096,256]{0,1:T(8,128)(2,1)} fusion(bf16[512,4096]{1,0:T(8,128)(2,1)} %param.8, bf16[512,256]{0,1:T(8,128)(2,1)} %all-reduce.12), kind=kOutput, calls=%fused_computation.6 | convolution fusion | flops 1074790400 | bytes 6553600 | tf_op jit(solution)/shard_map/dot_general | solution.py:72
  77.8 33.5 %reduce-scatter.2.cloned.1.call-done = bf16[4096,64]{0,1:T(8,128)(2,1)} async-done(((bf16[4096,256]{0,1:T(8,128)(2,1)}), bf16[4096,64]{0,1:T(8,128)(2,1)}) %reduce-scatter.2.cloned.1.call-update) | async-done | bytes 524304 | tf_op jit(solution)/shard_map/reduce_scatter | solution.py:75
  111.3 1.1 copy.28
  112.5 2.4 fusion.3
  114.8 1.2 broadcast_in_dim.5
  116.0 15.2 %scatter_fusion = f32[40,128,64]{1,2,0:T(8,128)} fusion(f32[40,128,64]{1,2,0:T(8,128)} %broadcast_in_dim.5, s32[96]{0:T(128)S(1)} %reshape.143, f32[96,128,64]{1,2,0:T(8,128)} %bitcast.88), kind=kCustom, calls=%fused_computation.2 | custom fusion | flops 786432 | bytes 9437568 | tf_op jit(solution)/shard_map/scatter-add | solution.py:54
  131.2 1.5 convert.11
  132.7 1.3 collective-permute-start.2
  134.1 3.0 collective-permute-start.3
  139.0 37.6 %all-gather.2.cloned.1.call-done = bf16[4096,256]{0,1:T(8,128)(2,1)} async-done(((bf16[4096,64]{0,1:T(8,128)(2,1)}), bf16[4096,256]{0,1:T(8,128)(2,1)}) %all-gather.2.cloned.1.call-update) | async-done | bytes 2097168 | tf_op jit(solution)/shard_map/all_gather | solution.py:79
  176.6 3.7 fusion.19
  180.5 55.3 %all-reduce.7.cloned.1.call-done = f32[256,256]{0,1:T(8,128)} async-done(((f32[256,256]{0,1:T(8,128)}), f32[256,256]{0,1:T(8,128)}) %all-reduce.7.cloned.1.call-update) | async-done | bytes 262160 | tf_op jit(solution)/shard_map/psum | solution.py:83
  235.9 1.7 broadcast_multiply_fusion
  240.3 11.7 %cholesky.50 = f32[128,128]{1,0:T(8,128)S(1)} custom-call(f32[128,128]{1,0:T(8,128)S(1)} %cholesky.118), custom_call_target="Cholesky" | custom-call | tf_op jit(solution)/shard_map/jit(cholesky)/cholesky | solution.py:84
  252.1 9.8 %custom-call.14 = f32[1,128,128]{1,2,0:T(8,128)S(1)} custom-call(f32[1,128,128]{2,1,0:T(8,128)S(1)} %get-tuple-element.60), custom_call_target="InvertDiagBlocksLowerTriangular" | custom-call | tf_op jit(solution)/shard_map/jit(cholesky)/cholesky | solution.py:84
  263.0 1.1 convolution_subtract_fusion.1
  264.1 11.7 %cholesky.105 = f32[128,128]{1,0:T(8,128)S(1)} custom-call(f32[128,128]{1,0:T(8,128)S(1)} %convolution_subtract_fusion.1), custom_call_target="Cholesky" | custom-call | tf_op jit(solution)/shard_map/jit(cholesky)/cholesky | solution.py:84
  278.8 5.5 %while.3 = (s32[]{:T(128)}, f32[256,256]{1,0:T(8,128)S(1)}, s32[2,2]{1,0:T(2,128)S(1)}, f32[2,128,128]{2,1,0:T(8,128)}, s32[]{:T(128)}) while((s32[]{:T(128)}, f32[256,256]{1,0:T(8,128)S(1)}, s32[2,2]{1,0:T(2,128)S(1)}, f32[2,128,128]{2,1,0:T(8,128)}, s32[]{:T(128)}) %tuple.41), condition=%wide.while_cond.2, body=%wide.while_body.2.sunk | while | flops 2 | bytes 132205 | solution.py:85
  279.6 2.0 bitcast_dynamic-update-slice_fusion.2
  282.2 2.0 bitcast_dynamic-update-slice_fusion.2
  284.3 20.5 %custom-call.15 = f32[2,128,128]{1,2,0:T(8,128)S(1)} custom-call(f32[2,128,128]{2,1,0:T(8,128)} %get-tuple-element.34), custom_call_target="InvertDiagBlocksLowerTriangular" | custom-call | tf_op jit(solution)/shard_map/triangular_solve | solution.py:85
  304.8 2.4 fusion.18
  307.2 2.1 convolution_subtract_fusion
  309.3 2.0 convolution_convert_fusion.1
  311.4 1.3 collective-permute-start.4
  312.7 1.3 collective-permute-start.5
  314.0 2.9 collective-permute-done.5
  316.9 3.7 pad_maximum_fusion.2
  320.6 4.4 copy.26
  325.0 7.8 %gather_fusion.1 = bf16[96,128,256]{2,1,0:T(8,128)(2,1)} fusion(bf16[40,128,256]{2,1,0:T(8,128)(2,1)} %bitcast.87, s32[1024]{0:T(1024)S(1)} %pad_clamp_fusion), kind=kCustom, calls=%fused_computation.1 | custom fusion | bytes 12583296 | tf_op jit(solution)/shard_map/gather | solution.py:43
  332.8 4.2 bitcast_convert_fusion
  337.0 1.3 copy-done.5
  338.3 2.1 convolution_bitcast_fusion
  340.5 60.1 %all-reduce.9.cloned.1.call-done = f32[512,256]{0,1:T(8,128)} async-done(((f32[512,256]{0,1:T(8,128)}), f32[512,256]{0,1:T(8,128)}) %all-reduce.9.cloned.1.call-update) | async-done | bytes 524304 | tf_op jit(solution)/shard_map/psum | solution.py:92
  400.5 2.5 convolution_convert_fusion.2
  403.0 3.1 pad_maximum_fusion
  406.1 4.1 copy.19
  410.2 34.9 %all-reduce.11.cloned.1.call-done = bf16[256,256]{1,0:T(8,128)(2,1)} async-done(((bf16[256,256]{1,0:T(8,128)(2,1)}), bf16[256,256]{1,0:T(8,128)(2,1)}) %all-reduce.11.cloned.1.call-update) | async-done | bytes 131088 | tf_op jit(solution)/shard_map/psum | solution.py:94
  445.1 1.6 convert_multiply_fusion
  (60 shorter events, 10.1 us)
Async XLA Ops:
  7.2 21.6 %copy-start = (bf16[32,3,128,128]{3,2,1,0:T(8,128)(2,1)S(1)}, bf16[32,3,128,128]{3,2,1,0:T(8,128)(2,1)}, u32[]{:S(2)}) copy-start(bf16[32,3,128,128]{3,2,1,0:T(8,128)(2,1)} %param.10) | copy-start | bytes 9437188
  7.2 104.1 %reduce-scatter.2.cloned.1.call-start = ((), (), s32[]{:S(2)}) async-start(), calls=%async_computation.1 | async-start | bytes 2621440 | tf_op jit(solution)/shard_map/reduce_scatter | solution.py:75
  9.2 5.3 %collective-permute-start = (bf16[512,256]{1,0:T(8,128)(2,1)}, bf16[512,256]{1,0:T(8,128)(2,1)}, u32[]{:S(2)}, u32[]{:S(2)}) collective-permute-start(bf16[512,256]{1,0:T(8,128)(2,1)} %get-tuple-element.53), channel_id=1, source_target_pairs={{0,1},{1,2},{2,3},{3,4},{4,5},{5,6},{6,7},{8,9},{9,10},{10,11},{11... | collective-permute-start | bytes 786440 | tf_op jit(solution)/shard_map/ppermute | solution.py:24
  12.3 5.3 %collective-permute-start.1 = (bf16[512,256]{1,0:T(8,128)(2,1)}, bf16[512,256]{1,0:T(8,128)(2,1)}, u32[]{:S(2)}, u32[]{:S(2)}) collective-permute-start(bf16[512,256]{1,0:T(8,128)(2,1)} %get-tuple-element.54), channel_id=1, source_target_pairs={{1,0},{2,1},{3,2},{4,3},{5,4},{6,5},{7,6},{9,8},{10,9},{11,10},{12... | collective-permute-start | bytes 786440 | tf_op jit(solution)/shard_map/ppermute | solution.py:26
  28.8 4.2 copy-start.8
  77.8 98.8 %all-gather.2.cloned.1.call-start = ((), (), s32[]{:S(2)}) async-start(), calls=%async_computation.2 | async-start | bytes 2621440 | tf_op jit(solution)/shard_map/all_gather | solution.py:79
  131.2 2.9 copy-start.1
  132.7 4.4 collective-permute-start.2
  134.1 3.9 collective-permute-start.3
  139.0 96.9 %all-reduce.7.cloned.1.call-start = ((), (), s32[]{:S(2)}) async-start(), calls=%async_computation.3 | async-start | bytes 524288 | tf_op jit(solution)/shard_map/psum | solution.py:83
  180.3 220.2 %all-reduce.9.cloned.1.call-start = ((), (), s32[]{:S(2)}) async-start(), calls=%async_computation.4 | async-start | bytes 1048576 | tf_op jit(solution)/shard_map/psum | solution.py:92
  239.6 0.7 copy-start.7
  275.8 1.9 copy-start.6
  304.8 2.4 copy-start.2
  307.2 9.7 %copy-start.4 = (bf16[4096,128]{0,1:T(8,128)(2,1)}, bf16[4096,128]{0,1:T(8,128)(2,1)S(1)}, u32[]{:S(2)}) copy-start(bf16[4096,128]{0,1:T(8,128)(2,1)S(1)} %get-tuple-element.63) | copy-start | bytes 3145732
  311.3 5.6 %copy-start.3 = (bf16[4096,128]{0,1:T(8,128)(2,1)}, bf16[4096,128]{0,1:T(8,128)(2,1)S(1)}, u32[]{:S(2)}) copy-start(bf16[4096,128]{0,1:T(8,128)(2,1)S(1)} %convolution_convert_fusion.1) | copy-start | bytes 3145732
  311.4 2.6 collective-permute-start.4
  312.7 4.2 collective-permute-start.5
  332.8 5.5 %copy-start.9 = (bf16[512,4096]{1,0:T(8,128)(2,1)S(1)}, bf16[512,4096]{1,0:T(8,128)(2,1)}, u32[]{:S(2)}) copy-start(bf16[512,4096]{1,0:T(8,128)(2,1)} %param.8) | copy-start | bytes 12582916
  337.0 1.3 copy-start.5
  340.4 104.7 %all-reduce.11.cloned.1.call-start = ((), (), s32[]{:S(2)}) async-start(), calls=%async_computation.5 | async-start | bytes 262144 | tf_op jit(solution)/shard_map/psum | solution.py:94
Sparse Core Ops, SparseCore 0:
  77.9 33.3 reduce-scatter.1
  139.1 37.4 all-gather.1
  180.4 55.4 all-reduce.6
  340.5 59.9 all-reduce.8
  403.8 41.2 all-reduce.10
where the time goes:
time: 454 us; the launch traced here: 453 us
  waiting for transfers between devices  228 us (50%)
  other arithmetic  88.3 us (19%)
  blocking collectives  37.8 us (8%)
  local copies, waits for them, and re-layouts  37.1 us (8%)
  matrix products  34.6 us (8%)
  between operations  15.3 us (3%)
  starting transfers between devices  11.7 us (3%)
    psum x1, waiting for transfers between devices, body(): projected = lax.psum(projected_part, 'par')  60.1 us
    psum x1, waiting for transfers between devices, body(): gram_matrix = lax.psum(gram_part, 'par') / total_par  55.3 us
    psum x1, blocking collectives, body(): forward = lax.psum(forward_part, 'par').astype(jnp.bfloat16)  37.8 us
    all_gather x1, waiting for transfers between devices, body(): lax.all_gather(sample_cols.astype(jnp.bfloat16), 'obs', axis=1, tiled=True)  37.6 us
    psum x1, waiting for transfers between devices, body(): lax.psum(ritz_part.astype(jnp.bfloat16), 'obs').astype(jnp.float32)  34.9 us
    another operation x6, other arithmetic, body(): lower_factor = jnp.linalg.cholesky(gram_matrix)  34 us
    reduce_scatter x1, waiting for transfers between devices, body(): lax.psum_scatter(adjoint_part.astype(jnp.bfloat16), 'obs', scatter_dimens...  33.5 us
    another operation x5, other arithmetic, body(): lax.linalg.triangular_solve(lower_factor, range_sample, left_side=False,...  24.6 us
  transfers between devices with their start and end apart: 11, of which 8 were waited for; matrix products, arithmetic and copies ran while one was open for 2% of the time, Pallas kernels for 0%

commit v1 on v0

v1 whole, which is shorter than its diff:
```python
import functools

import jax
import jax.numpy as jnp
from jax import lax
from jax.experimental import pallas as pl
from jax.experimental.pallas import tpu as pltpu
from jax.sharding import PartitionSpec as P

BLK = 128
REACH = 4
HALO = REACH * BLK
MESH = pl.DeviceIdType.MESH
F32 = jnp.float32
BF16 = jnp.bfloat16
VMEM = pl.BlockSpec(memory_space=pltpu.VMEM)
SMEM = pl.BlockSpec(memory_space=pltpu.SMEM)
LIMIT = 60 * 1024 * 1024


def greet(devices):
    barrier = pltpu.get_barrier_semaphore()
    for device in devices:
        pl.semaphore_signal(barrier, inc=1, device_id=device, device_id_type=MESH)
    pl.semaphore_wait(barrier, len(devices))


def remote(src, dst, send, recv, device):
    return pltpu.make_async_remote_copy(
        src_ref=src, dst_ref=dst, send_sem=send, recv_sem=recv, device_id=device, device_id_type=MESH
    )


def prior_block(b, base, source, coeffs, offs):
    def pick(offset):
        return source[b - base + offset]

    left = jnp.concatenate([coeffs[b, 0], coeffs[b, 1], coeffs[b, 2]], axis=1)
    right = jnp.concatenate([pick(0), pick(offs[b, 0]), pick(offs[b, 1])], axis=0)
    return jnp.dot(left, right, preferred_element_type=F32).astype(BF16)


def image_and_parts(n_par, o, p, offs, values, coeffs, jac, image, low, high, part, got, hs, hr, ps, pr):
    blocks = values.shape[0]
    side = 2 * REACH
    below = lax.rem(p + n_par - 1, n_par)
    above = lax.rem(p + 1, n_par)
    down = remote(values.at[pl.ds(0, REACH)], high.at[pl.ds(side, REACH)], hs.at[0], hr.at[0], (o, below))
    up = remote(values.at[pl.ds(blocks - REACH, REACH)], low.at[pl.ds(0, REACH)], hs.at[1], hr.at[1], (o, above))

    @pl.when(p > 0)
    def _():
        down.start()

    @pl.when(p < n_par - 1)
    def _():
        up.start()

    @pl.when(p == 0)
    def _():
        low[pl.ds(0, REACH)] = jnp.zeros((REACH,) + low.shape[1:], BF16)

    @pl.when(p == n_par - 1)
    def _():
        high[pl.ds(side, REACH)] = jnp.zeros((REACH,) + high.shape[1:], BF16)

    low[pl.ds(REACH, side)] = values[pl.ds(0, side)]
    high[pl.ds(0, side)] = values[pl.ds(blocks - side, side)]

    def inner(b, carry):
        image[pl.ds(pl.multiple_of(b * BLK, BLK), BLK), :] = prior_block(b, 0, values, coeffs, offs)
        return carry

    lax.fori_loop(REACH, blocks - REACH, inner, 0, unroll=4)

    @pl.when(p > 0)
    def _():
        down.wait_send()
        up.wait_recv()

    @pl.when(p < n_par - 1)
    def _():
        up.wait_send()
        down.wait_recv()

    for b in range(REACH):
        image[pl.ds(b * BLK, BLK), :] = prior_block(b, -REACH, low, coeffs, offs)
    for b in range(blocks - REACH, blocks):
        image[pl.ds(b * BLK, BLK), :] = prior_block(b, blocks - 2 * REACH, high, coeffs, offs)

    total = jnp.dot(jac[...], image[...], preferred_element_type=F32)
    piece = part.shape[1]
    for q in range(n_par):
        part[q] = total[q * piece : (q + 1) * piece].astype(BF16)
    copies = []
    for d in range(1, n_par):
        q = lax.rem(p + d, n_par)
        copy = remote(part.at[q], got.at[d], ps.at[d], pr.at[d], (o, q))
        copy.start()
        copies.append(copy)
    mine = part[p].astype(F32)
    for d in range(1, n_par):
        copies[d - 1].wait()
        mine = mine + got[d].astype(F32)
    return mine


def first_kernel(
    n_obs, n_par, offs, probes, coeffs, jac, out,
    image, low, high, part, got, fwd, adj, adj_got, hs, hr, ps, pr, gs, gr, os, orr,
):
    o, p = lax.axis_index("obs"), lax.axis_index("par")
    greet(
        [(o, lax.rem(p + d, n_par)) for d in range(1, n_par)]
        + [(lax.rem(o + d, n_obs), p) for d in range(1, n_obs)]
    )
    mine = image_and_parts(
        n_par, o, p, offs, probes, coeffs, jac, image, low, high, part, got, hs, hr, ps, pr
    )
    fwd[p] = mine.astype(BF16)
    copies = []
    for d in range(1, n_par):
        copy = remote(fwd.at[p], fwd.at[p], gs.at[d], gr.at[d], (o, lax.rem(p + d, n_par)))
        copy.start()
        copies.append(copy)
    for copy in copies:
        copy.wait()
    forward = fwd[...].reshape(jac.shape[0], fwd.shape[2])
    rows = adj.shape[1]
    tile = 256
    copies = []
    for d in list(range(1, n_obs)) + [0]:
        q = lax.rem(o + d, n_obs)

        def step(t, carry):
            start = pl.multiple_of(q * rows + t * tile, tile)
            value = lax.dot_general(
                jac[:, pl.ds(start, tile)], forward, (((0,), (0,)), ((), ())), preferred_element_type=F32
            )
            adj[d, pl.ds(pl.multiple_of(t * tile, tile), tile), :] = value.astype(BF16)
            return carry

        lax.fori_loop(0, rows // tile, step, 0)
        if d:
            copy = remote(adj.at[d], adj_got.at[d], os.at[d], orr.at[d], (q, p))
            copy.start()
            copies.append(copy)
    total = adj[0].astype(F32)
    for d in range(1, n_obs):
        copies[d - 1].wait()
        total = total + adj_got[d].astype(F32)
    out[...] = total.astype(BF16)


def adjoint_kernel(offs, values, coeffs, center, lower, upper, acc, held, sem):
    o = lax.axis_index("obs")
    blocks = values.shape[0] // BLK
    width = values.shape[1]
    load = pltpu.make_async_copy(coeffs.at[pl.ds(o * blocks, blocks)], held, sem.at[0])
    load.start()
    acc[...] = jnp.zeros_like(acc)
    load.wait()
    for b in range(blocks):
        v = values[pl.ds(b * BLK, BLK), :]
        for j in range(3):
            offset = 0 if j == 0 else offs[o * blocks + b, j - 1]
            where = pl.ds(pl.multiple_of((b + REACH + offset) * BLK, BLK), BLK)
            acc[where, :] += lax.dot_general(
                held[b, j], v, (((0,), (0,)), ((), ())), preferred_element_type=F32
            )
    lower[...] = acc[pl.ds(0, HALO), :].astype(BF16)
    center[...] = acc[pl.ds(HALO, blocks * BLK), :]
    upper[...] = acc[pl.ds(HALO + blocks * BLK, HALO), :].astype(BF16)


def everyone(n_obs, n_par, o, p):
    count = n_obs * n_par
    me = o * n_par + p
    others = []
    for d in range(1, count):
        k = lax.rem(me + d, count)
        others.append((k, (k // n_par, lax.rem(k, n_par))))
    return me, others


def sum_everywhere(me, others, value, send, got, out, ss, sr, gs, gr):
    count, piece, _ = send.shape
    for q in range(count):
        send[q] = value[q * piece : (q + 1) * piece]
    copies = []
    for d, (k, device) in enumerate(others, 1):
        copy = remote(send.at[k], got.at[d], ss.at[d], sr.at[d], device)
        copy.start()
        copies.append(copy)
    mine = send[me]
    for d, copy in enumerate(copies, 1):
        copy.wait()
        mine = mine + got[d]
    out[me] = mine
    copies = []
    for d, (k, device) in enumerate(others, 1):
        copy = remote(out.at[me], out.at[me], gs.at[d], gr.at[d], device)
        copy.start()
        copies.append(copy)
    return copies


def gram_kernel(
    n_obs, n_par, center, lower, upper, full, gram,
    sample, from_low, from_high, send, got, hs, hr, rs, rr, ss, sr, gs, gr,
):
    o, p = lax.axis_index("obs"), lax.axis_index("par")
    me, others = everyone(n_obs, n_par, o, p)
    greet([device for _, device in others])
    count = n_obs * n_par
    order = p * n_obs + o
    rows = center.shape[0]
    before = lax.rem(order + count - 1, count)
    after = lax.rem(order + 1, count)
    down = remote(lower, from_high, hs.at[0], hr.at[0], (lax.rem(before, n_obs), before // n_obs))
    up = remote(upper, from_low, hs.at[1], hr.at[1], (lax.rem(after, n_obs), after // n_obs))

    @pl.when(order > 0)
    def _():
        down.start()

    @pl.when(order < count - 1)
    def _():
        up.start()

    sample[...] = center[...]

    @pl.when(order > 0)
    def _():
        down.wait_send()
        up.wait_recv()
        sample[pl.ds(0, HALO), :] += from_low[...].astype(F32)

    @pl.when(order < count - 1)
    def _():
        up.wait_send()
        down.wait_recv()
        sample[pl.ds(rows - HALO, HALO), :] += from_high[...].astype(F32)

    full[o] = sample[...].astype(BF16)
    spread = []
    for d in range(1, n_obs):
        copy = remote(full.at[o], full.at[o], rs.at[d], rr.at[d], (lax.rem(o + d, n_obs), p))
        copy.start()
        spread.append(copy)
    value = lax.dot_general(
        sample[...], sample[...], (((0,), (0,)), ((), ())),
        precision=lax.Precision.HIGHEST, preferred_element_type=F32,
    ) / (rows * count)
    for copy in sum_everywhere(me, others, value, send, got, gram, ss, sr, gs, gr) + spread:
        copy.wait()


def second_kernel(
    n_obs, n_par, offs, basis, coeffs, jac, image, ritz,
    low, high, part, got, send, sum_got, hs, hr, ps, pr, ss, sr, gs, gr,
):
    o, p = lax.axis_index("obs"), lax.axis_index("par")
    me, others = everyone(n_obs, n_par, o, p)
    greet([device for _, device in others])
    mine = image_and_parts(
        n_par, o, p, offs, basis, coeffs, jac, image, low, high, part, got, hs, hr, ps, pr
    )
    value = lax.dot_general(
        mine, mine, (((0,), (0,)), ((), ())),
        precision=lax.Precision.HIGHEST, preferred_element_type=F32,
    ) / (jac.shape[0] * n_obs)
    for copy in sum_everywhere(me, others, value, send, sum_got, ritz, ss, sr, gs, gr):
        copy.wait()


def dma(count):
    return pltpu.SemaphoreType.DMA((count,))


def params(collective):
    return pltpu.CompilerParams(
        collective_id=collective, has_side_effects=True, vmem_limit_bytes=LIMIT
    )


def body(n_obs, n_par, jacobian, probes, coeffs, offsets):
    obs, rows = jacobian.shape
    width = probes.shape[1]
    own = rows // n_obs
    count = n_obs * n_par
    halos = [pltpu.VMEM((3 * REACH, BLK, width), BF16)] * 2
    parts = [pltpu.VMEM((n_par, obs // n_par, width), BF16)] * 2
    adjoint = pl.pallas_call(
        functools.partial(first_kernel, n_obs, n_par),
        out_shape=jax.ShapeDtypeStruct((own, width), BF16),
        in_specs=[SMEM, VMEM, VMEM, VMEM],
        out_specs=VMEM,
        scratch_shapes=[pltpu.VMEM((rows, width), BF16)]
        + halos
        + parts
        + [pltpu.VMEM((n_par, obs // n_par, width), BF16)]
        + [pltpu.VMEM((n_obs, own, width), BF16)] * 2
        + [dma(2)] * 2
        + [dma(n_par)] * 4
        + [dma(n_obs)] * 2,
        compiler_params=params(0),
        name="first_pass",
    )(offsets, probes.reshape(-1, BLK, width), coeffs, jacobian)
    center, lower, upper = pl.pallas_call(
        adjoint_kernel,
        out_shape=[
            jax.ShapeDtypeStruct((own, width), F32),
            jax.ShapeDtypeStruct((HALO, width), BF16),
            jax.ShapeDtypeStruct((HALO, width), BF16),
        ],
        in_specs=[SMEM, VMEM, pl.BlockSpec(memory_space=pl.ANY)],
        out_specs=[VMEM] * 3,
        scratch_shapes=[
            pltpu.VMEM((own + 2 * HALO, width), F32),
            pltpu.VMEM((own // BLK,) + coeffs.shape[1:], BF16),
            dma(1),
        ],
        compiler_params=pltpu.CompilerParams(vmem_limit_bytes=LIMIT),
        name="adjoint_prior",
    )(offsets, adjoint, coeffs)
    full, gram = pl.pallas_call(
        functools.partial(gram_kernel, n_obs, n_par),
        out_shape=[
            jax.ShapeDtypeStruct((n_obs, own, width), BF16),
            jax.ShapeDtypeStruct((count, width // count, width), F32),
        ],
        in_specs=[VMEM] * 3,
        out_specs=[VMEM] * 2,
        scratch_shapes=[pltpu.VMEM((own, width), F32)]
        + [pltpu.VMEM((HALO, width), BF16)] * 2
        + [pltpu.VMEM((count, width // count, width), F32)] * 2
        + [dma(2)] * 2
        + [dma(n_obs)] * 2
        + [dma(count)] * 4,
        compiler_params=params(1),
        name="gram",
    )(center, lower, upper)
    factor = jnp.linalg.cholesky(gram.reshape(width, width))
    inverse = lax.linalg.triangular_solve(
        factor, jnp.eye(width, dtype=F32), left_side=True, lower=True
    )
    high_part = inverse.astype(BF16)
    low_part = (inverse - high_part.astype(F32)).astype(BF16)
    sample = full.reshape(rows, width)
    last = (((1,), (1,)), ((), ()))
    basis = (
        lax.dot_general(sample, high_part, last, preferred_element_type=F32)
        + lax.dot_general(sample, low_part, last, preferred_element_type=F32)
    ).astype(BF16)
    image, ritz = pl.pallas_call(
        functools.partial(second_kernel, n_obs, n_par),
        out_shape=[
            jax.ShapeDtypeStruct((rows, width), BF16),
            jax.ShapeDtypeStruct((count, width // count, width), F32),
        ],
        in_specs=[SMEM, VMEM, VMEM, VMEM],
        out_specs=[VMEM] * 2,
        scratch_shapes=halos
        + parts
        + [pltpu.VMEM((count, width // count, width), F32)] * 2
        + [dma(2)] * 2
        + [dma(n_par)] * 2
        + [dma(count)] * 4,
        compiler_params=params(2),
        name="second_pass",
    )(offsets, basis.reshape(-1, BLK, width), coeffs, jacobian)
    return basis, image, ritz.reshape(width, width)


def solution(mesh):
    return jax.shard_map(
        functools.partial(body, mesh.shape["obs"], mesh.shape["par"]),
        mesh=mesh,
        in_specs=(P("obs", "par"), P("par", None), P("par", None, None, None), P("par", None)),
        out_specs=(P("par", None), P("par", None), P()),
        check_vma=False,
    )
```

time: 454 us -> 227 us (0.50)
  waiting for transfers between devices: 228 us -> 0 us
  Pallas kernels: 0 us -> 155 us
  blocking collectives: 37.8 us -> 0 us
  other arithmetic: 88.3 us -> 55 us
  matrix products: 34.6 us -> 4.15 us
  local copies, waits for them, and re-layouts: 37.1 us -> 10.3 us
  between operations: 15.3 us -> 2.1 us
  starting transfers between devices: 11.7 us -> 0 us
    pallas_call x0 -> x4, Pallas kernels: none -> 155 us  [the longest x1 56.9 us: body(): pl.pallas_call(functools.partial(gram_kernel, n_obs, n_par), out_shape=[j...]
    psum x3 -> x0, waiting for transfers between devices: 150 us -> none  [the longest x1 60.1 us: body(): projected = lax.psum(projected_part, 'par')]
    psum x1 -> x0, blocking collectives: 37.8 us -> none  [body(): forward = lax.psum(forward_part, 'par').astype(jnp.bfloat16)]
    all_gather x1 -> x0, waiting for transfers between devices: 37.6 us -> none  [body(): lax.all_gather(sample_cols.astype(jnp.bfloat16), 'obs', axis=1, tiled=True)]
    reduce_scatter x1 -> x0, waiting for transfers between devices: 33.5 us -> none  [body(): lax.psum_scatter(adjoint_part.astype(jnp.bfloat16), 'obs', scatter_dimens...]
    dot_general x8 -> x2, matrix products: 25.9 us -> 2.84 us  [the longest x1 2.1 us: body(): lax.dot_general(sample, low_part, last, preferred_element_type=F32)]
    gather x2 -> x0, local copies, waits for them, and re-layouts: 15.5 us -> none  [prior_forward(): picked = padded[positions]]
    scatter-add x3 -> x0, other arithmetic: 15.2 us -> none  [the longest x1 15.2 us: prior_adjoint(): jnp.zeros((count + 2 * REACH, BLK, width), jnp.float32).at[positions]]
  transfers between devices with their start and end apart: 11 -> 0, of which waited for: 8 -> 0; matrix products, arithmetic and copies ran while one was open for 2% -> 0% of each run, Pallas kernels for 0% -> 0%
where the time goes in v1:
time: 227 us
  Pallas kernels  155 us (68%)
  other arithmetic  55 us (24%)
  local copies, waits for them, and re-layouts  10.3 us (5%)
  matrix products  4.15 us (2%)
    pallas_call x1, Pallas kernels, body(): pl.pallas_call(functools.partial(gram_kernel, n_obs, n_par), out_shape=[j...  56.9 us
    pallas_call x1, Pallas kernels, body(): pl.pallas_call(functools.partial(first_kernel, n_obs, n_par), out_shape=j...  55 us
    pallas_call x1, Pallas kernels, body(): pl.pallas_call(functools.partial(second_kernel, n_obs, n_par), out_shape=...  39.1 us
    another operation x6, other arithmetic, body(): factor = jnp.linalg.cholesky(gram.reshape(width, width))  34.1 us
    another operation x3, other arithmetic, body(): lax.linalg.triangular_solve(factor, jnp.eye(width, dtype=F32), left_side=...  19.7 us
    unnamed x7, local copies, waits for them, and re-layouts  5.15 us

profile of v1, /device:TPU:0, one launch (start us, length us, event | category | flops | bytes accessed | tf_op | source)
XLA Modules:
  0.0 226.5 jit_solution(9614170134693504966)
XLA Ops:
  0.6 0.1 triangular_solve.63
  0.7 1.4 copy.13.offs
  2.1 55.0 %first_pass.1.values = bf16[1024,256]{1,0:T(8,128)(2,1)} custom-call(s32[32,2]{1,0:T(8,128)} %copy.13.offs, bf16[32,128,256]{2,1,0:T(8,128)(2,1)} %bitcast.42, bf16[32,3,128,128]{3,2,1,0:T(8,128)(2,1)} %coeffs.5, bf16[512,4096]{1,0:T(8,128)(2,1)} %jac.3), custom_call_target="tpu_custom_call" | custom-call | tf_op jit(solution)/shard_map/first_pass/pallas_call | solution.py:294
  57.1 4.0 %adjoint_prior.1 = (f32[1024,256]{1,0:T(8,128)}, bf16[512,256]{1,0:T(8,128)(2,1)}, bf16[512,256]{1,0:T(8,128)(2,1)}) custom-call(s32[32,2]{1,0:T(8,128)} %copy.13.offs, bf16[1024,256]{1,0:T(8,128)(2,1)} %first_pass.1.values, bf16[32,3,128,128]{3,2,1,0:T(8,128)(2,1)} %coeffs.5), custom_call_target="tpu_custom_call" | custom-call | tf_op jit(solution)/shard_map/adjoint_prior/pallas_call | solution.py:310
  61.1 56.9 %gram.1 = (bf16[4,1024,256]{2,1,0:T(8,128)(2,1)}, f32[32,8,256]{2,1,0:T(8,128)}) custom-call(f32[1024,256]{1,0:T(8,128)} %get-tuple-element.10.center, bf16[512,256]{1,0:T(8,128)(2,1)} %get-tuple-element.11.lower, bf16[512,256]{1,0:T(8,128)(2,1)} %get-tuple-element.12.upper), custom_call_target="tpu_custom_call" | custom-call | tf_op jit(solution)/shard_map/gram/pallas_call | solution.py:327
  118.0 1.1 copy.14
  119.1 0.0 copy-start
  119.1 1.1 fusion.1
  120.2 11.7 %cholesky.50 = f32[128,128]{1,0:T(8,128)S(1)} custom-call(f32[128,128]{1,0:T(8,128)S(1)} %cholesky.118), custom_call_target="Cholesky" | custom-call | tf_op jit(solution)/shard_map/jit(cholesky)/cholesky | solution.py:344
  132.0 9.8 %custom-call.14 = f32[1,128,128]{1,2,0:T(8,128)S(1)} custom-call(f32[1,128,128]{2,1,0:T(8,128)S(1)} %get-tuple-element.38), custom_call_target="InvertDiagBlocksLowerTriangular" | custom-call | tf_op jit(solution)/shard_map/jit(cholesky)/cholesky | solution.py:344
  141.8 0.2 constant_dynamic-update-slice_fusion.1
  142.1 0.3 convolution_subtract_fusion.1
  142.3 11.8 %cholesky.105 = f32[128,128]{1,0:T(8,128)S(1)} custom-call(f32[128,128]{1,0:T(8,128)S(1)} %convolution_subtract_fusion.1), custom_call_target="Cholesky" | custom-call | tf_op jit(solution)/shard_map/jit(cholesky)/cholesky | solution.py:344
  154.2 0.6 compare_reduce_fusion
  156.2 4.0 %while.1 = (s32[]{:T(128)}, f32[256,256]{1,0:T(8,128)S(1)}, s32[2,2]{1,0:T(2,128)S(1)}, f32[2,128,128]{2,1,0:T(8,128)S(1)}, s32[]{:T(128)}) while((s32[]{:T(128)}, f32[256,256]{1,0:T(8,128)S(1)}, s32[2,2]{1,0:T(2,128)S(1)}, f32[2,128,128]{2,1,0:T(8,128)S(1)}, s32[]{:T(128)}) %tuple.27), condition=%wide.while_cond, body=%wide.while_body.sunk | while | flops 2 | bytes 131189 | solution.py:345
  156.2 0.6 fusion.22
  156.8 1.4 bitcast_dynamic-update-slice_fusion.2
  158.2 0.6 fusion.22
  158.8 1.4 bitcast_dynamic-update-slice_fusion.2
  160.2 19.7 %custom-call.15 = f32[2,128,128]{1,2,0:T(8,128)S(1)} custom-call(f32[2,128,128]{2,1,0:T(8,128)S(1)} %get-tuple-element.24), custom_call_target="InvertDiagBlocksLowerTriangular" | custom-call | tf_op jit(solution)/shard_map/triangular_solve | solution.py:345
  179.9 0.3 fusion.5
  180.2 0.3 convolution_subtract_fusion
  180.4 0.3 fusion.8
  180.7 0.0 copy-done
  180.8 0.7 fusion.3
  181.5 2.1 fusion
  183.6 39.1 %second_pass.1 = (bf16[4096,256]{1,0:T(8,128)(2,1)}, f32[32,8,256]{2,1,0:T(8,128)}) custom-call(s32[32,2]{1,0:T(8,128)} %copy.13.offs, bf16[32,128,256]{2,1,0:T(8,128)(2,1)} %bitcast.41, bf16[32,3,128,128]{3,2,1,0:T(8,128)(2,1)} %coeffs.5, bf16[512,4096]{1,0:T(8,128)(2,1)} %jac.3), custom_call_target="tpu_custom_call" | custom-call | tf_op jit(solution)/shard_map/second_pass/pallas_call | solution.py:356
  222.7 0.0 copy-start.1
  222.7 3.1 %copy.30 = bf16[4096,256]{1,0:T(8,128)(2,1)} copy(bf16[4096,256]{1,0:T(8,128)(2,1)} %get-tuple-element.91) | data formatting | bytes 4194304
  225.8 0.0 copy-done.1
  225.8 0.7 copy.31
  (10 shorter events, 0.2 us)
Async XLA Ops:
  119.1 61.7 %copy-start = (bf16[4,1024,256]{2,1,0:T(8,128)(2,1)S(1)}, bf16[4,1024,256]{2,1,0:T(8,128)(2,1)}, u32[]{:S(2)}) copy-start(bf16[4,1024,256]{2,1,0:T(8,128)(2,1)} %get-tuple-element.13) | copy-start | bytes 6291460
  222.7 3.1 %copy-start.1 = (f32[32,8,256]{2,1,0:T(8,128)S(1)}, f32[32,8,256]{2,1,0:T(8,128)}, u32[]{:S(2)}) copy-start(f32[32,8,256]{2,1,0:T(8,128)} %get-tuple-element.16) | copy-start | bytes 786436

commit v2 on v1

--- a/solution.py
+++ b/solution.py
@@ -205,9 +205,60 @@
     return copies
 
 
+def small_inverse_factor(matrix):
+    size = matrix.shape[0]
+    row = lax.broadcasted_iota(jnp.int32, (size, size), 0)
+    lane = lax.broadcasted_iota(jnp.int32, (size, size), 1)
+    work = jnp.concatenate([matrix, (row == lane).astype(F32)], axis=1)
+    group = 8
+    parts = [work[g : g + group] for g in range(0, size, group)]
+    index = lax.broadcasted_iota(jnp.int32, (group, 2 * size), 0)
+    scales = []
+    for j in range(size):
+        first, at = j // group, j % group
+        columns = [jnp.broadcast_to(part[:, j : j + 1], part.shape) for part in parts[first:]]
+        pivot = columns[0][at : at + 1]
+        scales.append(lax.rsqrt(pivot))
+        scaled = parts[first][at : at + 1] * (1.0 / pivot)
+        for g, column in enumerate(columns):
+            if g == 0:
+                column = jnp.where(index > at, column, 0.0)
+            parts[first + g] = parts[first + g] - column * scaled
+    rows = [parts[j // group][j % group : j % group + 1] * scales[j] for j in range(size)]
+    return jnp.concatenate(rows, axis=0)[:, size:]
+
+
+def inverse_factor(gram, work, out, size):
+    blocks = work.shape[0]
+    width = blocks * size
+    row = lax.broadcasted_iota(jnp.int32, (size, width), 0)
+    lane = lax.broadcasted_iota(jnp.int32, (size, width), 1)
+    for k in range(blocks):
+        work[k, :, pl.ds(0, width)] = gram[k * size : (k + 1) * size]
+        work[k, :, pl.ds(width, width)] = (lane == row + k * size).astype(F32)
+
+    def step(k, carry):
+        rows = work[k]
+        shift = lax.rem(width - k * size, width)
+        diagonal = pltpu.roll(rows[:, :width], shift, 1)[:, :size]
+        small = small_inverse_factor(diagonal)
+        upper = jnp.dot(small, rows, precision=lax.Precision.HIGHEST, preferred_element_type=F32)
+        out[k] = upper[:, width:]
+        left = jnp.where(lane >= (k + 1) * size, upper[:, :width], 0.0)
+        update = lax.dot_general(
+            left, upper, (((0,), (0,)), ((), ())),
+            precision=lax.Precision.HIGHEST, preferred_element_type=F32,
+        )
+        for i in range(blocks):
+            work[i] -= update[i * size : (i + 1) * size]
+        return carry
+
+    lax.fori_loop(0, blocks, step, 0)
+
+
 def gram_kernel(
-    n_obs, n_par, center, lower, upper, full, gram,
-    sample, from_low, from_high, send, got, hs, hr, rs, rr, ss, sr, gs, gr,
+    n_obs, n_par, center, lower, upper, full, inverse,
+    sample, from_low, from_high, send, got, gram, work, hs, hr, rs, rr, ss, sr, gs, gr,
 ):
     o, p = lax.axis_index("obs"), lax.axis_index("par")
     me, others = everyone(n_obs, n_par, o, p)
@@ -243,16 +294,21 @@
         sample[pl.ds(rows - HALO, HALO), :] += from_high[...].astype(F32)
 
     full[o] = sample[...].astype(BF16)
+    value = lax.dot_general(
+        sample[...], sample[...], (((0,), (0,)), ((), ())),
+        precision=lax.Precision.HIGHEST, preferred_element_type=F32,
+    ) / (rows * count)
+    copies = sum_everywhere(me, others, value, send, got, gram, ss, sr, gs, gr)
     spread = []
     for d in range(1, n_obs):
         copy = remote(full.at[o], full.at[o], rs.at[d], rr.at[d], (lax.rem(o + d, n_obs), p))
         copy.start()
         spread.append(copy)
-    value = lax.dot_general(
-        sample[...], sample[...], (((0,), (0,)), ((), ())),
-        precision=lax.Precision.HIGHEST, preferred_element_type=F32,
-    ) / (rows * count)
-    for copy in sum_everywhere(me, others, value, send, got, gram, ss, sr, gs, gr) + spread:
+    for copy in copies:
+        copy.wait()
+    matrix = jnp.concatenate([gram[q] for q in range(count)], axis=0)
+    inverse_factor(matrix, work, inverse, inverse.shape[1])
+    for copy in spread:
         copy.wait()
 
 
@@ -324,27 +380,26 @@
         compiler_params=pltpu.CompilerParams(vmem_limit_bytes=LIMIT),
         name="adjoint_prior",
     )(offsets, adjoint, coeffs)
-    full, gram = pl.pallas_call(
+    block = 64
+    full, inverse = pl.pallas_call(
         functools.partial(gram_kernel, n_obs, n_par),
         out_shape=[
             jax.ShapeDtypeStruct((n_obs, own, width), BF16),
-            jax.ShapeDtypeStruct((count, width // count, width), F32),
+            jax.ShapeDtypeStruct((width // block, block, width), F32),
         ],
         in_specs=[VMEM] * 3,
         out_specs=[VMEM] * 2,
         scratch_shapes=[pltpu.VMEM((own, width), F32)]
         + [pltpu.VMEM((HALO, width), BF16)] * 2
-        + [pltpu.VMEM((count, width // count, width), F32)] * 2
+        + [pltpu.VMEM((count, width // count, width), F32)] * 3
+        + [pltpu.VMEM((width // block, block, 2 * width), F32)]
         + [dma(2)] * 2
         + [dma(n_obs)] * 2
         + [dma(count)] * 4,
         compiler_params=params(1),
         name="gram",
     )(center, lower, upper)
-    factor = jnp.linalg.cholesky(gram.reshape(width, width))
-    inverse = lax.linalg.triangular_solve(
-        factor, jnp.eye(width, dtype=F32), left_side=True, lower=True
-    )
+    inverse = inverse.reshape(width, width)
     high_part = inverse.astype(BF16)
     low_part = (inverse - high_part.astype(F32)).astype(BF16)
     sample = full.reshape(rows, width)

time: 227 us -> 180 us (0.79)
  other arithmetic: 55 us -> 1.07 us
  Pallas kernels: 155 us -> 169 us
  local copies, waits for them, and re-layouts: 10.3 us -> 5.16 us
    another operation x9 -> x0, other arithmetic: 53.8 us -> none  [the longest x6 34.1 us: body(): factor = jnp.linalg.cholesky(gram.reshape(width, width))]
    pallas_call x1, Pallas kernels: 56.9 us -> 64.2 us  [body(): pl.pallas_call(functools.partial(gram_kernel, n_obs, n_par), out_shape=[j...]
    pallas_call x1, Pallas kernels: 39.1 us -> 45.4 us  [body(): pl.pallas_call(functools.partial(second_kernel, n_obs, n_par), out_shape=...]
    another operation x9 -> x0, local copies, waits for them, and re-layouts: 4.05 us -> none
where the time goes in v2:
time: 180 us
  Pallas kernels  169 us (94%)
  local copies, waits for them, and re-layouts  5.16 us (3%)
  matrix products  4.54 us (3%)
    pallas_call x1, Pallas kernels, body(): pl.pallas_call(functools.partial(gram_kernel, n_obs, n_par), out_shape=[j...  64.2 us
    pallas_call x1, Pallas kernels, body(): pl.pallas_call(functools.partial(first_kernel, n_obs, n_par), out_shape=j...  54.9 us
    pallas_call x1, Pallas kernels, body(): pl.pallas_call(functools.partial(second_kernel, n_obs, n_par), out_shape=...  45.4 us
    unnamed x7, local copies, waits for them, and re-layouts  5.16 us
    pallas_call x1, Pallas kernels, body(): pl.pallas_call(adjoint_kernel, out_shape=[jax.ShapeDtypeStruct((own, widt...  3.98 us

profile of v2, /device:TPU:0, one launch (start us, length us, event | category | flops | bytes accessed | tf_op | source)
XLA Modules:
  0.0 180.0 jit_solution(2751722045674343636)
XLA Ops:
  0.6 1.4 copy.8.offs
  2.0 54.9 %first_pass.1.values = bf16[1024,256]{1,0:T(8,128)(2,1)} custom-call(s32[32,2]{1,0:T(8,128)} %copy.8.offs, bf16[32,128,256]{2,1,0:T(8,128)(2,1)} %bitcast.13, bf16[32,3,128,128]{3,2,1,0:T(8,128)(2,1)} %coeffs.5, bf16[512,4096]{1,0:T(8,128)(2,1)} %jac.3), custom_call_target="tpu_custom_call" | custom-call | tf_op jit(solution)/shard_map/first_pass/pallas_call | solution.py:350
  56.9 4.0 %adjoint_prior.1 = (f32[1024,256]{1,0:T(8,128)}, bf16[512,256]{1,0:T(8,128)(2,1)}, bf16[512,256]{1,0:T(8,128)(2,1)}) custom-call(s32[32,2]{1,0:T(8,128)} %copy.8.offs, bf16[1024,256]{1,0:T(8,128)(2,1)} %first_pass.1.values, bf16[32,3,128,128]{3,2,1,0:T(8,128)(2,1)} %coeffs.5), custom_call_target="tpu_custom_call" | custom-call | tf_op jit(solution)/shard_map/adjoint_prior/pallas_call | solution.py:366
  60.9 64.2 %gram.1 = (bf16[4,1024,256]{2,1,0:T(8,128)(2,1)}, f32[4,64,256]{2,1,0:T(8,128)}) custom-call(f32[1024,256]{1,0:T(8,128)} %get-tuple-element.10.center, bf16[512,256]{1,0:T(8,128)(2,1)} %get-tuple-element.11.lower, bf16[512,256]{1,0:T(8,128)(2,1)} %get-tuple-element.12.upper), custom_call_target="tpu_custom_call" | custom-call | tf_op jit(solution)/shard_map/gram/pallas_call | solution.py:384
  125.1 1.1 subtract_convert_fusion
  126.2 0.0 copy-start
  126.2 2.5 %fusion.1 = f32[4096,256]{1,0:T(8,128)S(1)} fusion(bf16[4096,256]{1,0:T(8,128)(2,1)} %bitcast.10, bf16[256,256]{1,0:T(8,128)(2,1)S(1)} %bitcast.15), kind=kOutput, calls=%fused_computation.3 | convolution fusion | flops 536870912 | bytes 6422528 | tf_op jit(solution)/shard_map/dot_general | solution.py:408
  128.7 0.0 copy-done
  128.7 2.1 %fusion = bf16[4096,256]{1,0:T(8,128)(2,1)} fusion(f32[4096,256]{1,0:T(8,128)S(1)} %fusion.1, bf16[4096,256]{1,0:T(8,128)(2,1)S(1)} %bitcast.11, bf16[256,256]{1,0:T(8,128)(2,1)S(1)} %bitcast.14), kind=kOutput, calls=%fused_computation.1 | convolution fusion | flops 538968064 | bytes 8519680 | tf_op jit(solution)/shard_map/dot_general | solution.py:409
  130.8 45.4 %second_pass.1 = (bf16[4096,256]{1,0:T(8,128)(2,1)}, f32[32,8,256]{2,1,0:T(8,128)}) custom-call(s32[32,2]{1,0:T(8,128)} %copy.8.offs, bf16[32,128,256]{2,1,0:T(8,128)(2,1)} %bitcast.12, bf16[32,3,128,128]{3,2,1,0:T(8,128)(2,1)} %coeffs.5, bf16[512,4096]{1,0:T(8,128)(2,1)} %jac.3), custom_call_target="tpu_custom_call" | custom-call | tf_op jit(solution)/shard_map/second_pass/pallas_call | solution.py:411
  176.2 0.0 copy-start.1
  176.2 3.1 %copy.12 = bf16[4096,256]{1,0:T(8,128)(2,1)} copy(bf16[4096,256]{1,0:T(8,128)(2,1)} %get-tuple-element.23) | data formatting | bytes 4194304
  179.3 0.0 copy-done.1
  179.3 0.7 copy.13
Async XLA Ops:
  126.2 2.5 %copy-start = (bf16[4,1024,256]{2,1,0:T(8,128)(2,1)S(1)}, bf16[4,1024,256]{2,1,0:T(8,128)(2,1)}, u32[]{:S(2)}) copy-start(bf16[4,1024,256]{2,1,0:T(8,128)(2,1)} %get-tuple-element.13) | copy-start | bytes 6291460
  176.2 3.1 %copy-start.1 = (f32[32,8,256]{2,1,0:T(8,128)S(1)}, f32[32,8,256]{2,1,0:T(8,128)}, u32[]{:S(2)}) copy-start(f32[32,8,256]{2,1,0:T(8,128)} %get-tuple-element.16) | copy-start | bytes 786436

commit v3 on v2

--- a/solution.py
+++ b/solution.py
@@ -40,13 +40,30 @@
     return jnp.dot(left, right, preferred_element_type=F32).astype(BF16)
 
 
-def image_and_parts(n_par, o, p, offs, values, coeffs, jac, image, low, high, part, got, hs, hr, ps, pr):
+def fetch(source, coeffs, jac, values, held, jac_held, low, high, sem):
+    blocks = source.shape[0]
+    side = 2 * REACH
+    loads = [
+        pltpu.make_async_copy(source, values, sem.at[0]),
+        pltpu.make_async_copy(coeffs, held, sem.at[1]),
+        pltpu.make_async_copy(source.at[pl.ds(0, side)], low.at[pl.ds(REACH, side)], sem.at[2]),
+        pltpu.make_async_copy(source.at[pl.ds(blocks - side, side)], high.at[pl.ds(0, side)], sem.at[3]),
+        pltpu.make_async_copy(jac, jac_held, sem.at[4]),
+    ]
+    for load in loads:
+        load.start()
+    return loads
+
+
+def image_and_parts(
+    n_par, o, p, offs, source, loads, values, coeffs, jac, image, low, high, part, got, hs, hr, ps, pr
+):
     blocks = values.shape[0]
     side = 2 * REACH
     below = lax.rem(p + n_par - 1, n_par)
     above = lax.rem(p + 1, n_par)
-    down = remote(values.at[pl.ds(0, REACH)], high.at[pl.ds(side, REACH)], hs.at[0], hr.at[0], (o, below))
-    up = remote(values.at[pl.ds(blocks - REACH, REACH)], low.at[pl.ds(0, REACH)], hs.at[1], hr.at[1], (o, above))
+    down = remote(source.at[pl.ds(0, REACH)], high.at[pl.ds(side, REACH)], hs.at[0], hr.at[0], (o, below))
+    up = remote(source.at[pl.ds(blocks - REACH, REACH)], low.at[pl.ds(0, REACH)], hs.at[1], hr.at[1], (o, above))
 
     @pl.when(p > 0)
     def _():
@@ -64,8 +81,8 @@
     def _():
         high[pl.ds(side, REACH)] = jnp.zeros((REACH,) + high.shape[1:], BF16)
 
-    low[pl.ds(REACH, side)] = values[pl.ds(0, side)]
-    high[pl.ds(0, side)] = values[pl.ds(blocks - side, side)]
+    loads[0].wait()
+    loads[1].wait()
 
     def inner(b, carry):
         image[pl.ds(pl.multiple_of(b * BLK, BLK), BLK), :] = prior_block(b, 0, values, coeffs, offs)
@@ -83,11 +100,14 @@
         up.wait_send()
         down.wait_recv()
 
+    loads[2].wait()
+    loads[3].wait()
     for b in range(REACH):
         image[pl.ds(b * BLK, BLK), :] = prior_block(b, -REACH, low, coeffs, offs)
     for b in range(blocks - REACH, blocks):
         image[pl.ds(b * BLK, BLK), :] = prior_block(b, blocks - 2 * REACH, high, coeffs, offs)
 
+    loads[4].wait()
     total = jnp.dot(jac[...], image[...], preferred_element_type=F32)
     piece = part.shape[1]
     for q in range(n_par):
@@ -106,16 +126,18 @@
 
 
 def first_kernel(
-    n_obs, n_par, offs, probes, coeffs, jac, out,
-    image, low, high, part, got, fwd, adj, adj_got, hs, hr, ps, pr, gs, gr, os, orr,
+    n_obs, n_par, offs, probes, coeffs, jac_ref, out,
+    low, high, values, held, jac, ls, image, part, got, fwd, adj, adj_got, hs, hr, ps, pr, gs, gr, os, orr,
 ):
     o, p = lax.axis_index("obs"), lax.axis_index("par")
+    loads = fetch(probes, coeffs, jac_ref, values, held, jac, low, high, ls)
     greet(
         [(o, lax.rem(p + d, n_par)) for d in range(1, n_par)]
         + [(lax.rem(o + d, n_obs), p) for d in range(1, n_obs)]
     )
     mine = image_and_parts(
-        n_par, o, p, offs, probes, coeffs, jac, image, low, high, part, got, hs, hr, ps, pr
+        n_par, o, p, offs, probes, loads, values, held, jac, image, low, high,
+        part, got, hs, hr, ps, pr,
     )
     fwd[p] = mine.astype(BF16)
     copies = []
@@ -173,36 +195,65 @@
     upper[...] = acc[pl.ds(HALO + blocks * BLK, HALO), :].astype(BF16)
 
 
-def everyone(n_obs, n_par, o, p):
-    count = n_obs * n_par
-    me = o * n_par + p
-    others = []
-    for d in range(1, count):
-        k = lax.rem(me + d, count)
-        others.append((k, (k // n_par, lax.rem(k, n_par))))
-    return me, others
-
-
-def sum_everywhere(me, others, value, send, got, out, ss, sr, gs, gr):
-    count, piece, _ = send.shape
-    for q in range(count):
-        send[q] = value[q * piece : (q + 1) * piece]
+def groups(n_obs, n_par, o, p):
+    along_obs = [(lax.rem(o + d, n_obs), p) for d in range(1, n_obs)]
+    along_par = [(o, lax.rem(p + d, n_par)) for d in range(1, n_par)]
+    return along_obs, along_par
+
+
+def swap(send, got, index, devices, send_sem, recv_sem):
     copies = []
-    for d, (k, device) in enumerate(others, 1):
-        copy = remote(send.at[k], got.at[d], ss.at[d], sr.at[d], device)
-        copy.start()
-        copies.append(copy)
-    mine = send[me]
-    for d, copy in enumerate(copies, 1):
-        copy.wait()
-        mine = mine + got[d]
-    out[me] = mine
-    copies = []
-    for d, (k, device) in enumerate(others, 1):
-        copy = remote(out.at[me], out.at[me], gs.at[d], gr.at[d], device)
+    for d, device in enumerate(devices, 1):
+        copy = remote(send.at[device[index]], got.at[d], send_sem.at[d], recv_sem.at[d], device)
         copy.start()
         copies.append(copy)
     return copies
+
+
+def spread_out(ref, devices, send_sem, recv_sem):
+    copies = []
+    for d, device in enumerate(devices, 1):
+        copy = remote(ref, ref, send_sem.at[d], recv_sem.at[d], device)
+        copy.start()
+        copies.append(copy)
+    return copies
+
+
+def sum_everywhere(o, p, devices, value, send1, got1, send2, got2, out, sems):
+    along_obs, along_par = devices
+    n_obs, n_par, piece, _ = out.shape
+    kind = out.dtype
+    tall = n_par * piece
+    for q in range(n_obs):
+        send1[q] = value[q * tall : (q + 1) * tall].astype(kind)
+    copies = swap(send1, got1, 0, along_obs, sems[0], sems[1])
+    mine = send1[o].astype(F32)
+    for d, copy in enumerate(copies, 1):
+        copy.wait()
+        mine = mine + got1[d].astype(F32)
+    for q in range(n_par):
+        send2[q] = mine[q * piece : (q + 1) * piece].astype(kind)
+    copies = swap(send2, got2, 1, along_par, sems[2], sems[3])
+    mine = send2[p].astype(F32)
+    for d, copy in enumerate(copies, 1):
+        copy.wait()
+        mine = mine + got2[d].astype(F32)
+    out[o, p] = mine.astype(kind)
+    for copy in spread_out(out.at[o, p], along_par, sems[4], sems[5]):
+        copy.wait()
+    for copy in spread_out(out.at[o], along_obs, sems[6], sems[7]):
+        copy.wait()
+
+
+def sum_scratch(n_obs, n_par, width, kind):
+    tall = width // n_obs
+    return (
+        [pltpu.VMEM((n_obs, tall, width), kind)] * 2
+        + [pltpu.VMEM((n_par, tall // n_par, width), kind)] * 2
+        + [dma(n_obs)] * 2
+        + [dma(n_par)] * 4
+        + [dma(n_obs)] * 2
+    )
 
 
 def small_inverse_factor(matrix):
@@ -214,16 +265,23 @@
     parts = [work[g : g + group] for g in range(0, size, group)]
     index = lax.broadcasted_iota(jnp.int32, (group, 2 * size), 0)
     scales = []
-    for j in range(size):
-        first, at = j // group, j % group
-        columns = [jnp.broadcast_to(part[:, j : j + 1], part.shape) for part in parts[first:]]
-        pivot = columns[0][at : at + 1]
-        scales.append(lax.rsqrt(pivot))
-        scaled = parts[first][at : at + 1] * (1.0 / pivot)
-        for g, column in enumerate(columns):
-            if g == 0:
-                column = jnp.where(index > at, column, 0.0)
-            parts[first + g] = parts[first + g] - column * scaled
+    for first in range(size // group):
+        start = first * group
+        columns = [
+            [jnp.broadcast_to(part[:, start + t : start + t + 1], part.shape) for part in parts[first:]]
+            for t in range(group)
+        ]
+        for t in range(group):
+            pivot = columns[t][0][t : t + 1]
+            scales.append(lax.rsqrt(pivot))
+            reciprocal = 1.0 / pivot
+            scaled = parts[first][t : t + 1] * reciprocal
+            columns[t][0] = jnp.where(index > t, columns[t][0], 0.0)
+            for u in range(t + 1, group):
+                ratio = columns[u][0][t : t + 1] * reciprocal
+                columns[u] = [c - e * ratio for c, e in zip(columns[u], columns[t])]
+            for g, column in enumerate(columns[t]):
+                parts[first + g] = parts[first + g] - column * scaled
     rows = [parts[j // group][j % group : j % group + 1] * scales[j] for j in range(size)]
     return jnp.concatenate(rows, axis=0)[:, size:]
 
@@ -258,18 +316,20 @@
 
 def gram_kernel(
     n_obs, n_par, center, lower, upper, full, inverse,
-    sample, from_low, from_high, send, got, gram, work, hs, hr, rs, rr, ss, sr, gs, gr,
+    sample, from_low, from_high, gram, work, hs, hr, rs, rr, send1, got1, send2, got2, *sems,
 ):
     o, p = lax.axis_index("obs"), lax.axis_index("par")
-    me, others = everyone(n_obs, n_par, o, p)
-    greet([device for _, device in others])
+    devices = groups(n_obs, n_par, o, p)
     count = n_obs * n_par
     order = p * n_obs + o
     rows = center.shape[0]
     before = lax.rem(order + count - 1, count)
     after = lax.rem(order + 1, count)
-    down = remote(lower, from_high, hs.at[0], hr.at[0], (lax.rem(before, n_obs), before // n_obs))
-    up = remote(upper, from_low, hs.at[1], hr.at[1], (lax.rem(after, n_obs), after // n_obs))
+    below = (lax.rem(before, n_obs), before // n_obs)
+    above = (lax.rem(after, n_obs), after // n_obs)
+    greet(devices[0] + devices[1] + [below, above])
+    down = remote(lower, from_high, hs.at[0], hr.at[0], below)
+    up = remote(upper, from_low, hs.at[1], hr.at[1], above)
 
     @pl.when(order > 0)
     def _():
@@ -298,15 +358,11 @@
         sample[...], sample[...], (((0,), (0,)), ((), ())),
         precision=lax.Precision.HIGHEST, preferred_element_type=F32,
     ) / (rows * count)
-    copies = sum_everywhere(me, others, value, send, got, gram, ss, sr, gs, gr)
-    spread = []
-    for d in range(1, n_obs):
-        copy = remote(full.at[o], full.at[o], rs.at[d], rr.at[d], (lax.rem(o + d, n_obs), p))
-        copy.start()
-        spread.append(copy)
-    for copy in copies:
-        copy.wait()
-    matrix = jnp.concatenate([gram[q] for q in range(count)], axis=0)
+    sum_everywhere(o, p, devices, value, send1, got1, send2, got2, gram, sems)
+    spread = spread_out(full.at[o], devices[0], rs, rr)
+    matrix = jnp.concatenate(
+        [gram[i, q] for i in range(n_obs) for q in range(n_par)], axis=0
+    )
     inverse_factor(matrix, work, inverse, inverse.shape[1])
     for copy in spread:
         copy.wait()
@@ -314,20 +370,27 @@
 
 def second_kernel(
     n_obs, n_par, offs, basis, coeffs, jac, image, ritz,
-    low, high, part, got, send, sum_got, hs, hr, ps, pr, ss, sr, gs, gr,
+    low, high, values, held, jac_held, ls, part, got, total, hs, hr, ps, pr,
+    send1, got1, send2, got2, *sems,
 ):
     o, p = lax.axis_index("obs"), lax.axis_index("par")
-    me, others = everyone(n_obs, n_par, o, p)
-    greet([device for _, device in others])
+    loads = fetch(basis, coeffs, jac, values, held, jac_held, low, high, ls)
+    devices = groups(n_obs, n_par, o, p)
+    greet(devices[0] + devices[1])
     mine = image_and_parts(
-        n_par, o, p, offs, basis, coeffs, jac, image, low, high, part, got, hs, hr, ps, pr
+        n_par, o, p, offs, basis, loads, values, held, jac_held, image, low, high,
+        part, got, hs, hr, ps, pr,
     )
     value = lax.dot_general(
         mine, mine, (((0,), (0,)), ((), ())),
         precision=lax.Precision.HIGHEST, preferred_element_type=F32,
-    ) / (jac.shape[0] * n_obs)
-    for copy in sum_everywhere(me, others, value, send, sum_got, ritz, ss, sr, gs, gr):
-        copy.wait()
+    ) / (jac_held.shape[0] * n_obs)
+    sum_everywhere(o, p, devices, value, send1, got1, send2, got2, total, sems)
+    piece = total.shape[2]
+    for i in range(n_obs):
+        for q in range(n_par):
+            start = (i * n_par + q) * piece
+            ritz[start : start + piece, :] = total[i, q].astype(F32)
 
 
 def dma(count):
@@ -345,15 +408,21 @@
     width = probes.shape[1]
     own = rows // n_obs
     count = n_obs * n_par
-    halos = [pltpu.VMEM((3 * REACH, BLK, width), BF16)] * 2
+    halos = [pltpu.VMEM((3 * REACH, BLK, width), BF16)] * 2 + [
+        pltpu.VMEM((rows // BLK, BLK, width), BF16),
+        pltpu.VMEM(coeffs.shape, BF16),
+        pltpu.VMEM((obs, rows), BF16),
+        dma(5),
+    ]
+    anywhere = pl.BlockSpec(memory_space=pl.ANY)
     parts = [pltpu.VMEM((n_par, obs // n_par, width), BF16)] * 2
     adjoint = pl.pallas_call(
         functools.partial(first_kernel, n_obs, n_par),
         out_shape=jax.ShapeDtypeStruct((own, width), BF16),
-        in_specs=[SMEM, VMEM, VMEM, VMEM],
+        in_specs=[SMEM, anywhere, anywhere, anywhere],
         out_specs=VMEM,
-        scratch_shapes=[pltpu.VMEM((rows, width), BF16)]
-        + halos
+        scratch_shapes=halos
+        + [pltpu.VMEM((rows, width), BF16)]
         + parts
         + [pltpu.VMEM((n_par, obs // n_par, width), BF16)]
         + [pltpu.VMEM((n_obs, own, width), BF16)] * 2
@@ -391,11 +460,11 @@
         out_specs=[VMEM] * 2,
         scratch_shapes=[pltpu.VMEM((own, width), F32)]
         + [pltpu.VMEM((HALO, width), BF16)] * 2
-        + [pltpu.VMEM((count, width // count, width), F32)] * 3
+        + [pltpu.VMEM((n_obs, n_par, width // count, width), F32)]
         + [pltpu.VMEM((width // block, block, 2 * width), F32)]
         + [dma(2)] * 2
         + [dma(n_obs)] * 2
-        + [dma(count)] * 4,
+        + sum_scratch(n_obs, n_par, width, F32),
         compiler_params=params(1),
         name="gram",
     )(center, lower, upper)
@@ -412,20 +481,20 @@
         functools.partial(second_kernel, n_obs, n_par),
         out_shape=[
             jax.ShapeDtypeStruct((rows, width), BF16),
-            jax.ShapeDtypeStruct((count, width // count, width), F32),
+            jax.ShapeDtypeStruct((width, width), F32),
         ],
-        in_specs=[SMEM, VMEM, VMEM, VMEM],
+        in_specs=[SMEM, anywhere, anywhere, anywhere],
         out_specs=[VMEM] * 2,
         scratch_shapes=halos
         + parts
-        + [pltpu.VMEM((count, width // count, width), F32)] * 2
+        + [pltpu.VMEM((n_obs, n_par, width // count, width), BF16)]
         + [dma(2)] * 2
         + [dma(n_par)] * 2
-        + [dma(count)] * 4,
+        + sum_scratch(n_obs, n_par, width, BF16),
         compiler_params=params(2),
         name="second_pass",
     )(offsets, basis.reshape(-1, BLK, width), coeffs, jacobian)
-    return basis, image, ritz.reshape(width, width)
+    return basis, image, ritz
 
 
 def solution(mesh):

time: 180 us -> 164 us (0.911)
  Pallas kernels: 169 us -> 153 us
    pallas_call x1, Pallas kernels: 45.4 us -> 33.6 us  [body(): pl.pallas_call(functools.partial(second_kernel, n_obs, n_par), out_shape=...]
    pallas_call x1, Pallas kernels: 54.9 us -> 52.4 us  [body(): pl.pallas_call(functools.partial(first_kernel, n_obs, n_par), out_shape=j...]
where the time goes in v3:
time: 164 us
  Pallas kernels  153 us (93%)
  local copies, waits for them, and re-layouts  5.16 us (3%)
  matrix products  4.54 us (3%)
    pallas_call x1, Pallas kernels, body(): pl.pallas_call(functools.partial(gram_kernel, n_obs, n_par), out_shape=[j...  62.7 us
    pallas_call x1, Pallas kernels, body(): pl.pallas_call(functools.partial(first_kernel, n_obs, n_par), out_shape=j...  52.4 us
    pallas_call x1, Pallas kernels, body(): pl.pallas_call(functools.partial(second_kernel, n_obs, n_par), out_shape=...  33.6 us
    unnamed x7, local copies, waits for them, and re-layouts  5.16 us
    pallas_call x1, Pallas kernels, body(): pl.pallas_call(adjoint_kernel, out_shape=[jax.ShapeDtypeStruct((own, widt...  3.98 us

profile of v3, /device:TPU:0, one launch (start us, length us, event | category | flops | bytes accessed | tf_op | source)
XLA Modules:
  0.0 164.0 jit_solution(1467737104487134022)
XLA Ops:
  0.6 1.4 copy.8.offs
  2.0 52.4 %first_pass.1.values = bf16[1024,256]{1,0:T(8,128)(2,1)} custom-call(s32[32,2]{1,0:T(8,128)} %copy.8.offs, bf16[32,128,256]{2,1,0:T(8,128)(2,1)} %bitcast.12, bf16[32,3,128,128]{3,2,1,0:T(8,128)(2,1)} %coeffs.5, bf16[512,4096]{1,0:T(8,128)(2,1)} %jac.1), custom_call_target="tpu_custom_call" | custom-call | tf_op jit(solution)/shard_map/first_pass/pallas_call | solution.py:419
  54.4 4.0 %adjoint_prior.1 = (f32[1024,256]{1,0:T(8,128)}, bf16[512,256]{1,0:T(8,128)(2,1)}, bf16[512,256]{1,0:T(8,128)(2,1)}) custom-call(s32[32,2]{1,0:T(8,128)} %copy.8.offs, bf16[1024,256]{1,0:T(8,128)(2,1)} %first_pass.1.values, bf16[32,3,128,128]{3,2,1,0:T(8,128)(2,1)} %coeffs.5), custom_call_target="tpu_custom_call" | custom-call | tf_op jit(solution)/shard_map/adjoint_prior/pallas_call | solution.py:435
  58.4 62.7 %gram.1 = (bf16[4,1024,256]{2,1,0:T(8,128)(2,1)}, f32[4,64,256]{2,1,0:T(8,128)}) custom-call(f32[1024,256]{1,0:T(8,128)} %get-tuple-element.10.center, bf16[512,256]{1,0:T(8,128)(2,1)} %get-tuple-element.11.lower, bf16[512,256]{1,0:T(8,128)(2,1)} %get-tuple-element.12.upper), custom_call_target="tpu_custom_call" | custom-call | tf_op jit(solution)/shard_map/gram/pallas_call | solution.py:453
  121.0 1.1 subtract_convert_fusion
  122.1 0.0 copy-start
  122.1 2.5 %fusion.1 = f32[4096,256]{1,0:T(8,128)S(1)} fusion(bf16[4096,256]{1,0:T(8,128)(2,1)} %bitcast.9, bf16[256,256]{1,0:T(8,128)(2,1)S(1)} %bitcast.14), kind=kOutput, calls=%fused_computation.3 | convolution fusion | flops 536870912 | bytes 6422528 | tf_op jit(solution)/shard_map/dot_general | solution.py:477
  124.6 0.0 copy-done
  124.6 2.1 %fusion = bf16[4096,256]{1,0:T(8,128)(2,1)} fusion(f32[4096,256]{1,0:T(8,128)S(1)} %fusion.1, bf16[4096,256]{1,0:T(8,128)(2,1)S(1)} %bitcast.10, bf16[256,256]{1,0:T(8,128)(2,1)S(1)} %bitcast.13), kind=kOutput, calls=%fused_computation.1 | convolution fusion | flops 538968064 | bytes 8519680 | tf_op jit(solution)/shard_map/dot_general | solution.py:478
  126.7 33.6 %second_pass.1 = (bf16[4096,256]{1,0:T(8,128)(2,1)}, f32[256,256]{1,0:T(8,128)}) custom-call(s32[32,2]{1,0:T(8,128)} %copy.8.offs, bf16[32,128,256]{2,1,0:T(8,128)(2,1)} %bitcast.11, bf16[32,3,128,128]{3,2,1,0:T(8,128)(2,1)} %coeffs.5, bf16[512,4096]{1,0:T(8,128)(2,1)} %jac.1), custom_call_target="tpu_custom_call" | custom-call | tf_op jit(solution)/shard_map/second_pass/pallas_call | solution.py:480
  160.2 0.0 copy-start.1
  160.2 3.1 %copy.12 = bf16[4096,256]{1,0:T(8,128)(2,1)} copy(bf16[4096,256]{1,0:T(8,128)(2,1)} %get-tuple-element.23) | data formatting | bytes 4194304
  163.3 0.0 copy-done.1
  163.3 0.7 copy.13
Async XLA Ops:
  122.1 2.5 %copy-start = (bf16[4,1024,256]{2,1,0:T(8,128)(2,1)S(1)}, bf16[4,1024,256]{2,1,0:T(8,128)(2,1)}, u32[]{:S(2)}) copy-start(bf16[4,1024,256]{2,1,0:T(8,128)(2,1)} %get-tuple-element.13) | copy-start | bytes 6291460
  160.2 3.1 %copy-start.1 = (f32[256,256]{1,0:T(8,128)S(1)}, f32[256,256]{1,0:T(8,128)}, u32[]{:S(2)}) copy-start(f32[256,256]{1,0:T(8,128)} %get-tuple-element.24) | copy-start | bytes 786436

commit v4 on v3

--- a/solution.py
+++ b/solution.py
@@ -219,7 +219,7 @@
     return copies
 
 
-def sum_everywhere(o, p, devices, value, send1, got1, send2, got2, out, sems):
+def sum_everywhere(o, p, devices, value, send1, got1, send2, got2, out, sems, beside=None):
     along_obs, along_par = devices
     n_obs, n_par, piece, _ = out.shape
     kind = out.dtype
@@ -231,6 +231,8 @@
     for d, copy in enumerate(copies, 1):
         copy.wait()
         mine = mine + got1[d].astype(F32)
+    if beside is not None:
+        beside()
     for q in range(n_par):
         send2[q] = mine[q * piece : (q + 1) * piece].astype(kind)
     copies = swap(send2, got2, 1, along_par, sems[2], sems[3])
@@ -358,8 +360,18 @@
         sample[...], sample[...], (((0,), (0,)), ((), ())),
         precision=lax.Precision.HIGHEST, preferred_element_type=F32,
     ) / (rows * count)
-    sum_everywhere(o, p, devices, value, send1, got1, send2, got2, gram, sems)
-    spread = spread_out(full.at[o], devices[0], rs, rr)
+    spread = []
+    half = rows // 2
+
+    def send_half(h):
+        spread.extend(
+            spread_out(full.at[o, pl.ds(h * half, half)], devices[0], rs.at[h], rr.at[h])
+        )
+
+    sum_everywhere(
+        o, p, devices, value, send1, got1, send2, got2, gram, sems, lambda: send_half(0)
+    )
+    send_half(1)
     matrix = jnp.concatenate(
         [gram[i, q] for i in range(n_obs) for q in range(n_par)], axis=0
     )
@@ -463,7 +475,7 @@
         + [pltpu.VMEM((n_obs, n_par, width // count, width), F32)]
         + [pltpu.VMEM((width // block, block, 2 * width), F32)]
         + [dma(2)] * 2
-        + [dma(n_obs)] * 2
+        + [pltpu.SemaphoreType.DMA((2, n_obs))] * 2
         + sum_scratch(n_obs, n_par, width, F32),
         compiler_params=params(1),
         name="gram",

time: 164 us -> 156 us (0.951)
  Pallas kernels: 153 us -> 144 us
    pallas_call x1, Pallas kernels: 62.7 us -> 54.1 us  [body(): pl.pallas_call(functools.partial(gram_kernel, n_obs, n_par), out_shape=[j...]
where the time goes in v4:
time: 156 us; the launch traced here: 155 us
  Pallas kernels  144 us (92%)
  local copies, waits for them, and re-layouts  5.16 us (3%)
  matrix products  4.54 us (3%)
    pallas_call x1, Pallas kernels, body(): pl.pallas_call(functools.partial(gram_kernel, n_obs, n_par), out_shape=[j...  54.1 us
    pallas_call x1, Pallas kernels, body(): pl.pallas_call(functools.partial(first_kernel, n_obs, n_par), out_shape=j...  52.4 us
    pallas_call x1, Pallas kernels, body(): pl.pallas_call(functools.partial(second_kernel, n_obs, n_par), out_shape=...  33.2 us
    unnamed x7, local copies, waits for them, and re-layouts  5.16 us
    pallas_call x1, Pallas kernels, body(): pl.pallas_call(adjoint_kernel, out_shape=[jax.ShapeDtypeStruct((own, widt...  3.98 us

profile of v4, /device:TPU:0, one launch (start us, length us, event | category | flops | bytes accessed | tf_op | source)
XLA Modules:
  0.0 155.2 jit_solution(5050035675405237419)
XLA Ops:
  0.6 1.4 copy.8.offs
  2.0 52.4 %first_pass.1.values = bf16[1024,256]{1,0:T(8,128)(2,1)} custom-call(s32[32,2]{1,0:T(8,128)} %copy.8.offs, bf16[32,128,256]{2,1,0:T(8,128)(2,1)} %bitcast.12, bf16[32,3,128,128]{3,2,1,0:T(8,128)(2,1)} %coeffs.5, bf16[512,4096]{1,0:T(8,128)(2,1)} %jac.1), custom_call_target="tpu_custom_call" | custom-call | tf_op jit(solution)/shard_map/first_pass/pallas_call | solution.py:431
  54.4 4.0 %adjoint_prior.1 = (f32[1024,256]{1,0:T(8,128)}, bf16[512,256]{1,0:T(8,128)(2,1)}, bf16[512,256]{1,0:T(8,128)(2,1)}) custom-call(s32[32,2]{1,0:T(8,128)} %copy.8.offs, bf16[1024,256]{1,0:T(8,128)(2,1)} %first_pass.1.values, bf16[32,3,128,128]{3,2,1,0:T(8,128)(2,1)} %coeffs.5), custom_call_target="tpu_custom_call" | custom-call | tf_op jit(solution)/shard_map/adjoint_prior/pallas_call | solution.py:447
  58.4 54.1 %gram.1 = (bf16[4,1024,256]{2,1,0:T(8,128)(2,1)}, f32[4,64,256]{2,1,0:T(8,128)}) custom-call(f32[1024,256]{1,0:T(8,128)} %get-tuple-element.10.center, bf16[512,256]{1,0:T(8,128)(2,1)} %get-tuple-element.11.lower, bf16[512,256]{1,0:T(8,128)(2,1)} %get-tuple-element.12.upper), custom_call_target="tpu_custom_call" | custom-call | tf_op jit(solution)/shard_map/gram/pallas_call | solution.py:465
  112.5 1.1 subtract_convert_fusion
  113.6 0.0 copy-start
  113.6 2.5 %fusion.1 = f32[4096,256]{1,0:T(8,128)S(1)} fusion(bf16[4096,256]{1,0:T(8,128)(2,1)} %bitcast.9, bf16[256,256]{1,0:T(8,128)(2,1)S(1)} %bitcast.14), kind=kOutput, calls=%fused_computation.3 | convolution fusion | flops 536870912 | bytes 6422528 | tf_op jit(solution)/shard_map/dot_general | solution.py:489
  116.0 0.0 copy-done
  116.1 2.1 %fusion = bf16[4096,256]{1,0:T(8,128)(2,1)} fusion(f32[4096,256]{1,0:T(8,128)S(1)} %fusion.1, bf16[4096,256]{1,0:T(8,128)(2,1)S(1)} %bitcast.10, bf16[256,256]{1,0:T(8,128)(2,1)S(1)} %bitcast.13), kind=kOutput, calls=%fused_computation.1 | convolution fusion | flops 538968064 | bytes 8519680 | tf_op jit(solution)/shard_map/dot_general | solution.py:490
  118.1 33.2 %second_pass.1 = (bf16[4096,256]{1,0:T(8,128)(2,1)}, f32[256,256]{1,0:T(8,128)}) custom-call(s32[32,2]{1,0:T(8,128)} %copy.8.offs, bf16[32,128,256]{2,1,0:T(8,128)(2,1)} %bitcast.11, bf16[32,3,128,128]{3,2,1,0:T(8,128)(2,1)} %coeffs.5, bf16[512,4096]{1,0:T(8,128)(2,1)} %jac.1), custom_call_target="tpu_custom_call" | custom-call | tf_op jit(solution)/shard_map/second_pass/pallas_call | solution.py:492
  151.4 0.0 copy-start.1
  151.4 3.1 %copy.12 = bf16[4096,256]{1,0:T(8,128)(2,1)} copy(bf16[4096,256]{1,0:T(8,128)(2,1)} %get-tuple-element.23) | data formatting | bytes 4194304
  154.5 0.0 copy-done.1
  154.5 0.7 copy.13
Async XLA Ops:
  113.6 2.5 %copy-start = (bf16[4,1024,256]{2,1,0:T(8,128)(2,1)S(1)}, bf16[4,1024,256]{2,1,0:T(8,128)(2,1)}, u32[]{:S(2)}) copy-start(bf16[4,1024,256]{2,1,0:T(8,128)(2,1)} %get-tuple-element.13) | copy-start | bytes 6291460
  151.4 3.1 %copy-start.1 = (f32[256,256]{1,0:T(8,128)S(1)}, f32[256,256]{1,0:T(8,128)}, u32[]{:S(2)}) copy-start(f32[256,256]{1,0:T(8,128)} %get-tuple-element.24) | copy-start | bytes 786436

commit v5 on v4

--- a/solution.py
+++ b/solution.py
@@ -108,16 +108,25 @@
         image[pl.ds(b * BLK, BLK), :] = prior_block(b, blocks - 2 * REACH, high, coeffs, offs)
 
     loads[4].wait()
-    total = jnp.dot(jac[...], image[...], preferred_element_type=F32)
     piece = part.shape[1]
-    for q in range(n_par):
-        part[q] = total[q * piece : (q + 1) * piece].astype(BF16)
-    copies = []
-    for d in range(1, n_par):
-        q = lax.rem(p + d, n_par)
-        copy = remote(part.at[q], got.at[d], ps.at[d], pr.at[d], (o, q))
-        copy.start()
-        copies.append(copy)
+    half = n_par // 2
+
+    def to(q, d):
+        return remote(part.at[q], got.at[d], ps.at[d], pr.at[d], (o, q))
+
+    for first in (0, half):
+        total = jnp.dot(
+            jac[first * piece : (first + half) * piece, :], image[...], preferred_element_type=F32
+        )
+        for q in range(half):
+            part[first + q] = total[q * piece : (q + 1) * piece].astype(BF16)
+        for q in range(first, first + half):
+
+            @pl.when(p != q)
+            def _():
+                to(q, lax.rem(q - p + n_par, n_par)).start()
+
+    copies = [to(lax.rem(p + d, n_par), d) for d in range(1, n_par)]
     mine = part[p].astype(F32)
     for d in range(1, n_par):
         copies[d - 1].wait()

time: 156 us -> 156 us (level)
  no operation moved by 1% of the time
where the time goes in v5:
time: 156 us
  Pallas kernels  144 us (92%)
  local copies, waits for them, and re-layouts  5.16 us (3%)
  matrix products  4.55 us (3%)
    pallas_call x1, Pallas kernels, body(): pl.pallas_call(functools.partial(gram_kernel, n_obs, n_par), out_shape=[j...  53.4 us
    pallas_call x1, Pallas kernels, body(): pl.pallas_call(functools.partial(first_kernel, n_obs, n_par), out_shape=j...  53.3 us
    pallas_call x1, Pallas kernels, body(): pl.pallas_call(functools.partial(second_kernel, n_obs, n_par), out_shape=...  33.8 us
    unnamed x7, local copies, waits for them, and re-layouts  5.16 us
    pallas_call x1, Pallas kernels, body(): pl.pallas_call(adjoint_kernel, out_shape=[jax.ShapeDtypeStruct((own, widt...  3.98 us

profile of v5, /device:TPU:0, one launch (start us, length us, event | category | flops | bytes accessed | tf_op | source)
XLA Modules:
  0.0 155.9 jit_solution(15634134169006031338)
XLA Ops:
  0.6 1.4 copy.8.offs
  2.0 53.3 %first_pass.1.values = bf16[1024,256]{1,0:T(8,128)(2,1)} custom-call(s32[32,2]{1,0:T(8,128)} %copy.8.offs, bf16[32,128,256]{2,1,0:T(8,128)(2,1)} %bitcast.12, bf16[32,3,128,128]{3,2,1,0:T(8,128)(2,1)} %coeffs.5, bf16[512,4096]{1,0:T(8,128)(2,1)} %jac.1), custom_call_target="tpu_custom_call" | custom-call | tf_op jit(solution)/shard_map/first_pass/pallas_call | solution.py:440
  55.3 4.0 %adjoint_prior.1 = (f32[1024,256]{1,0:T(8,128)}, bf16[512,256]{1,0:T(8,128)(2,1)}, bf16[512,256]{1,0:T(8,128)(2,1)}) custom-call(s32[32,2]{1,0:T(8,128)} %copy.8.offs, bf16[1024,256]{1,0:T(8,128)(2,1)} %first_pass.1.values, bf16[32,3,128,128]{3,2,1,0:T(8,128)(2,1)} %coeffs.5), custom_call_target="tpu_custom_call" | custom-call | tf_op jit(solution)/shard_map/adjoint_prior/pallas_call | solution.py:456
  59.2 53.4 %gram.1 = (bf16[4,1024,256]{2,1,0:T(8,128)(2,1)}, f32[4,64,256]{2,1,0:T(8,128)}) custom-call(f32[1024,256]{1,0:T(8,128)} %get-tuple-element.10.center, bf16[512,256]{1,0:T(8,128)(2,1)} %get-tuple-element.11.lower, bf16[512,256]{1,0:T(8,128)(2,1)} %get-tuple-element.12.upper), custom_call_target="tpu_custom_call" | custom-call | tf_op jit(solution)/shard_map/gram/pallas_call | solution.py:474
  112.6 1.1 subtract_convert_fusion
  113.7 0.0 copy-start
  113.7 2.5 %fusion.1 = f32[4096,256]{1,0:T(8,128)S(1)} fusion(bf16[4096,256]{1,0:T(8,128)(2,1)} %bitcast.9, bf16[256,256]{1,0:T(8,128)(2,1)S(1)} %bitcast.14), kind=kOutput, calls=%fused_computation.3 | convolution fusion | flops 536870912 | bytes 6422528 | tf_op jit(solution)/shard_map/dot_general | solution.py:498
  116.2 0.0 copy-done
  116.2 2.1 %fusion = bf16[4096,256]{1,0:T(8,128)(2,1)} fusion(f32[4096,256]{1,0:T(8,128)S(1)} %fusion.1, bf16[4096,256]{1,0:T(8,128)(2,1)S(1)} %bitcast.10, bf16[256,256]{1,0:T(8,128)(2,1)S(1)} %bitcast.13), kind=kOutput, calls=%fused_computation.1 | convolution fusion | flops 538968064 | bytes 8519680 | tf_op jit(solution)/shard_map/dot_general | solution.py:499
  118.3 33.8 %second_pass.1 = (bf16[4096,256]{1,0:T(8,128)(2,1)}, f32[256,256]{1,0:T(8,128)}) custom-call(s32[32,2]{1,0:T(8,128)} %copy.8.offs, bf16[32,128,256]{2,1,0:T(8,128)(2,1)} %bitcast.11, bf16[32,3,128,128]{3,2,1,0:T(8,128)(2,1)} %coeffs.5, bf16[512,4096]{1,0:T(8,128)(2,1)} %jac.1), custom_call_target="tpu_custom_call" | custom-call | tf_op jit(solution)/shard_map/second_pass/pallas_call | solution.py:501
  152.1 0.0 copy-start.1
  152.1 3.1 %copy.12 = bf16[4096,256]{1,0:T(8,128)(2,1)} copy(bf16[4096,256]{1,0:T(8,128)(2,1)} %get-tuple-element.23) | data formatting | bytes 4194304
  155.2 0.0 copy-done.1
  155.2 0.7 copy.13
Async XLA Ops:
  113.7 2.5 %copy-start = (bf16[4,1024,256]{2,1,0:T(8,128)(2,1)S(1)}, bf16[4,1024,256]{2,1,0:T(8,128)(2,1)}, u32[]{:S(2)}) copy-start(bf16[4,1024,256]{2,1,0:T(8,128)(2,1)} %get-tuple-element.13) | copy-start | bytes 6291460
  152.1 3.1 %copy-start.1 = (f32[256,256]{1,0:T(8,128)S(1)}, f32[256,256]{1,0:T(8,128)}, u32[]{:S(2)}) copy-start(f32[256,256]{1,0:T(8,128)} %get-tuple-element.24) | copy-start | bytes 786436
